TPU v7x, 512 devices: a whole 4x4x16 slice. The times are simulated.
512 devices in a mesh: tile: 32 (over z, core), chan: 16 (over y, x).
Axes of the slice: x: 4, y: 4, z: 16, core: 2. Of those that a mesh axis runs over, the one named last changes fastest.
Arguments:
- fields: float32 [64, 1024, 411], P('chan', 'tile'), may hold values from -12 to 12
- diffusivity: float32 [64, 1024], P('chan', 'tile'), may hold values from 0.02 to 0.24
- owners: int32 [4096, 1], replicated, may hold values from 0 to 31; in each aligned block of 128 rows (0 to 127, 128 to 255, ...) at most 8 rows name the same one
- observed: bfloat16 [8192, 6144], P('tile', 'chan'), may hold values from -6 to 6
- usable: int32 [8192], P('tile'), may hold values 0 or 1
- w_hidden: bfloat16 [411, 2048], P(None, 'chan'), may hold values from -0.3125 to 0.3125
- b_hidden: float32 [2048], P('chan'), may hold values from -3 to 3
- w_radiance: bfloat16 [2048, 6144], P(None, 'chan'), may hold values from -0.125 to 0.125
- b_radiance: float32 [6144], P('chan'), may hold values from -3 to 3
- inv_cov: bfloat16 [6144, 6144], P('tile', 'chan'), may hold values from -6 to 22
Outputs:
- gradient: float32 [64, 1024, 411], P('chan', 'tile')
Inputs may be any that keep to these rules, and one draw needn't show every extreme that they name: `owners`: in each tile's block of 128 consecutive entries no owner appears more than 8 times, and in some blocks one appears exactly 8 times.
All inputs are finite; a program needn't handle non-finite values. No bound on the sum of `usable` on one device may be relied on, other than what follows from the above.
Results may differ from a plain program's by a relative error of at most 0.0045.
Values may be sent and summed in bfloat16 or wider, within the bound.
A program may use at most 64 MiB of HBM per device.

v0:
```python
import jax
import jax.numpy as jnp
from jax import lax
from jax.sharding import PartitionSpec as P


def padded_2(value, sides, width, wrap):
    for axis, dim in sides:
        devices, length = (lax.axis_size(axis), value.shape[dim])
        up = [(i, (i + 1) % devices) for i in range(devices if wrap else devices - 1)]
        down = [(j, i) for i, j in up]
        last = lax.slice_in_dim(value, length - width, length, axis=dim)
        first = lax.slice_in_dim(value, 0, width, axis=dim)
        before = lax.ppermute(last, axis, up)
        after = lax.ppermute(first, axis, down)
        value = jnp.concatenate([before, value, after], axis=dim)
    return value


def add_rims(values):
    rowwise = padded_2(values, (("chan", 0),), 1, False)
    return padded_2(rowwise, (("tile", 1),), 1, True)


def body(
    fields,
    diffusivity,
    owners,
    observed,
    usable,
    w_hidden,
    b_hidden,
    w_radiance,
    b_radiance,
    inv_cov,
):
    tile_count = lax.axis_size("tile")
    chan_count = lax.axis_size("chan")
    tile_index = lax.axis_index("tile")
    chan_index = lax.axis_index("chan")
    slot_count = observed.shape[0]
    capacity = slot_count // tile_count
    cells_across, cells_along, features = fields.shape
    own_cols = cells_across // 4 * (cells_along // 4)
    tile_cols = chan_count * own_cols
    hidden_dev = w_hidden.shape[1]
    owner_table = owners[:, 0].reshape(tile_count, tile_cols)
    owner_hits = (
        owner_table[:, :, None] == jnp.arange(tile_count, dtype=jnp.int32)[None, None, :]
    ).astype(jnp.int32)
    before = jnp.sum((jnp.cumsum(owner_hits, axis=1) - owner_hits) * owner_hits, axis=2)
    tallies = jnp.sum(owner_hits, axis=1)
    slot_of = lax.dynamic_index_in_dim(
        owner_table * capacity + before, tile_index, 0, keepdims=False
    )
    arriving = lax.dynamic_index_in_dim(tallies, tile_index, 1, keepdims=False)
    occupied = (jnp.arange(capacity, dtype=jnp.int32)[None, :] < arriving[:, None]).reshape(
        slot_count
    )
    grouped = fields.reshape(cells_across // 4, 4, cells_along // 4, 4, features)
    columns = (
        (jnp.sum(grouped, axis=(1, 3)) * 0.0625).reshape(own_cols, features).astype(jnp.bfloat16)
    )
    placer = (slot_of[None, :] == jnp.arange(slot_count, dtype=jnp.int32)[:, None]).astype(
        jnp.bfloat16
    )
    picks = placer
    outgoing = jnp.dot(
        picks,
        lax.all_gather(columns, "chan", axis=0, tiled=True),
        preferred_element_type=jnp.float32,
    )
    incoming = lax.all_to_all(
        outgoing.astype(jnp.bfloat16), "tile", split_axis=0, concat_axis=0, tiled=True
    )
    preact = lax.dot_general(
        w_hidden, incoming, (((0,), (1,)), ((), ())), preferred_element_type=jnp.float32
    )
    preact = preact + b_hidden[:, None]
    squash = jax.nn.sigmoid(preact)
    active = (preact * squash).astype(jnp.bfloat16)
    weights = w_radiance
    radiance = lax.dot_general(
        lax.all_gather(active, "chan", axis=0, tiled=True),
        weights,
        (((0,), (0,)), ((), ())),
        preferred_element_type=jnp.float32,
    )
    radiance = radiance + b_radiance[None, :]
    in_use = usable.astype(jnp.float32) * occupied.astype(jnp.float32)
    departure = ((radiance - observed.astype(jnp.float32)) * in_use[:, None]).astype(jnp.bfloat16)
    all_depart = lax.all_gather(departure, "chan", axis=1, tiled=True)
    picks = all_depart
    cotangent = jnp.dot(
        picks,
        lax.all_gather(inv_cov, "tile", axis=0, tiled=True),
        preferred_element_type=jnp.float32,
    )
    cotangent = cotangent.astype(jnp.bfloat16)
    weights = w_radiance
    full_sum = lax.psum(
        lax.dot_general(
            weights, cotangent, (((1,), (1,)), ((), ())), preferred_element_type=jnp.float32
        ),
        "chan",
    )
    grad_hidden = lax.dynamic_slice_in_dim(full_sum, chan_index * hidden_dev, hidden_dev, 0)
    slope_term = squash * (1.0 + preact * (1.0 - squash))
    grad_pre = (grad_hidden * slope_term).astype(jnp.bfloat16)
    part_grad = lax.dot_general(
        grad_pre, w_hidden, (((0,), (1,)), ((), ())), preferred_element_type=jnp.float32
    )
    summed_grad = lax.psum(part_grad, "chan")
    returned = lax.all_to_all(summed_grad, "tile", split_axis=0, concat_axis=0, tiled=True)
    own_slots = lax.dynamic_slice_in_dim(slot_of, chan_index * own_cols, own_cols, 0)
    column_grad = jnp.take(returned, own_slots, axis=0)
    spread = jnp.repeat(
        column_grad.reshape(cells_across // 4, cells_along // 4, features), 4, axis=0
    )
    adjoint = jnp.repeat(spread, 4, axis=1) * 0.0625
    kappa_root = jnp.sqrt(diffusivity)
    root_rim = add_rims(kappa_root)
    coef_north = (kappa_root * root_rim[2:, 1:-1])[:, :, None]
    coef_south = (kappa_root * root_rim[:-2, 1:-1])[:, :, None]
    coef_east = (kappa_root * root_rim[1:-1, 2:])[:, :, None]
    coef_west = (kappa_root * root_rim[1:-1, :-2])[:, :, None]
    for sweep_index in range(2):
        padded = add_rims(adjoint)
        adjoint = (
            adjoint
            + coef_north * (padded[2:, 1:-1] - adjoint)
            + coef_south * (padded[:-2, 1:-1] - adjoint)
            + coef_east * (padded[1:-1, 2:] - adjoint)
            + coef_west * (padded[1:-1, :-2] - adjoint)
        )
    return adjoint


def solution(mesh):
    placed = (
        P("chan", "tile", None),
        P("chan", "tile"),
        P(),
        P("tile", "chan"),
        P("tile"),
        P(None, "chan"),
        P("chan"),
        P(None, "chan"),
        P("chan"),
        P("tile", "chan"),
    )
    return jax.shard_map(
        body, mesh=mesh, in_specs=placed, out_specs=P("chan", "tile", None), check_vma=False
    )
```

profile of v0, /device:TPU:6, one launch (start us, length us, event | category | flops | bytes accessed | tf_op | source)
XLA Modules:
  0.0 599.1 jit_solution(5220718163068988109)
XLA Ops:
  6.6 0.0 all-gather.4.cloned.1.call-start
  6.6 0.9 copy.26
  7.5 1.0 reduce_sum.35
  8.6 3.3 convert_reduce_fusion
  12.0 26.5 %all_gather.12 = bf16[128,411]{1,0:T(8,128)(2,1)S(1)} all-gather(bf16[8,411]{1,0:T(8,128)(2,1)S(1)} %multiply_convert_fusion.3), channel_id=1, replica_groups=mesh['tile'=32,'chan'=16] {'chan'}, dimensions={0}, use_global_device_ids=true | all-gather | bytes 111792 | tf_op jit(solution)/shard_map/all_gather | solution.py:70
  38.5 0.2 dynamic-slice_reduce_fusion
  38.6 0.3 convolution_convert_fusion
  38.9 0.1 copy.29
  39.1 35.1 %all_to_all.24 = bf16[32,8,411]{2,1,0:T(8,128)(2,1)S(1)} all-to-all(bf16[32,8,411]{2,1,0:T(8,128)(2,1)S(1)} %bitcast.26), channel_id=1, replica_groups=mesh['tile'=32,'chan'=16] {'tile'}, dimensions={0} | all-to-all | bytes 420864 | tf_op jit(solution)/shard_map/all_to_all | solution.py:73
  74.2 0.9 multiply_convert_fusion.1
  75.1 0.0 all-gather.4.cloned.1.call-update
  75.1 0.0 all-gather.6.cloned.1.call-start
  75.2 0.2 dynamic-slice_reduce_fusion.1
  75.3 0.1 iota_compare_fusion.4
  75.4 0.1 lt.53
  75.5 47.4 %all-gather.4.cloned.1.call-done = bf16[2048,256]{0,1:T(8,128)(2,1)} async-done(((bf16[128,256]{0,1:T(8,128)(2,1)}), bf16[2048,256]{0,1:T(8,128)(2,1)}) %all-gather.4.cloned.1.call-update) | async-done | bytes 1048592 | tf_op jit(solution)/shard_map/all_gather | solution.py:84
  122.9 2.6 fusion.6
  125.5 0.0 all-gather.6.cloned.1.call-update
  125.6 0.0 all-gather.8.cloned.1.call-start
  125.6 0.7 all-gather.8.cloned.1.call-update
  126.3 0.0 all-reduce.3.cloned.1.call-start
  126.3 66.2 %all-gather.6.cloned.1.call-done = bf16[256,6144]{1,0:T(8,128)(2,1)} async-done(((bf16[256,384]{1,0:T(8,128)(2,1)}), bf16[256,6144]{1,0:T(8,128)(2,1)}) %all-gather.6.cloned.1.call-update) | async-done | bytes 3145744 | tf_op jit(solution)/shard_map/all_gather | solution.py:92
  192.5 75.9 %all-gather.8.cloned.1.call-done = bf16[6144,384]{1,0:T(8,128)(2,1)} async-done(((bf16[192,384]{1,0:T(8,128)(2,1)}), bf16[6144,384]{1,0:T(8,128)(2,1)}) %all-gather.8.cloned.1.call-update) | async-done | bytes 4718608 | tf_op jit(solution)/shard_map/all_gather | solution.py:96
  268.4 7.1 %convolution_bitcast_fusion = f32[2048,256]{0,1:T(8,128)} fusion(bf16[2048,384]{1,0:T(8,128)(2,1)S(1)} %copy-done, bf16[256,6144]{1,0:T(8,128)(2,1)} %all-gather.6.cloned.1.call-done, bf16[6144,384]{1,0:T(8,128)(2,1)} %all-gather.8.cloned.1.call-done), kind=kOutput, calls=%fused_computation.5 | convolution fusion | flops 1610711040 | bytes 11534336 | tf_op jit(solution)/shard_map/dot_general | solution.py:102
  275.5 0.0 all-reduce.3.cloned.1.call-update
  275.5 0.0 all-reduce.5.cloned.1.call-start
  275.6 118.8 %all-reduce.3.cloned.1.call-done = f32[2048,256]{0,1:T(8,128)} async-done(((f32[2048,256]{0,1:T(8,128)}), f32[2048,256]{0,1:T(8,128)}) %all-reduce.3.cloned.1.call-update) | async-done | bytes 2097168 | tf_op jit(solution)/shard_map/psum | solution.py:101
  394.4 2.0 convolution_bitcast_fusion.1
  396.3 0.0 all-reduce.5.cloned.1.call-update
  396.3 117.1 %all-reduce.5.cloned.1.call-done = f32[32,8,411]{2,1,0:T(8,128)} async-done(((f32[32,8,411]{2,1,0:T(8,128)}), f32[32,8,411]{2,1,0:T(8,128)}) %all-reduce.5.cloned.1.call-update) | async-done | bytes 420880 | tf_op jit(solution)/shard_map/psum | solution.py:113
  513.4 12.6 %all-to-all-start.1 = ((f32[32,8,411]{2,1,0:T(8,128)}), f32[32,8,411]{2,1,0:T(8,128)S(1)}, u32[]{:S(2)}, u32[]{:S(2)}) async-start(f32[32,8,411]{2,1,0:T(8,128)} %all-reduce.5.cloned.1.call-done), calls=%async_computation.1 | async-start | bytes 1048576 | tf_op jit(solution)/shard_map/all_to_all | solution.py:114
  526.1 3.4 collective-permute-start.2
  529.4 2.5 collective-permute-start
  531.9 0.2 dynamic-slice_reduce_fusion.2
  532.1 0.0 collective-permute-done.2
  532.2 4.8 collective-permute-done
  537.0 0.1 fusion.40
  537.1 1.7 collective-permute-start.4
  538.8 0.0 collective-permute-start.6
  538.8 21.3 %all-to-all-done.1 = f32[32,8,411]{2,1,0:T(8,128)S(1)} async-done(((f32[32,8,411]{2,1,0:T(8,128)}), f32[32,8,411]{2,1,0:T(8,128)S(1)}, u32[]{:S(2)}, u32[]{:S(2)}) %all-to-all-start.1) | async-done | bytes 420896 | tf_op jit(solution)/shard_map/all_to_all | solution.py:114
  560.0 0.6 gather_fusion
  560.6 0.1 select_multiply_fusion
  560.7 3.4 collective-permute-start.3
  564.1 2.5 collective-permute-start.1
  566.6 0.0 collective-permute-done.4
  566.6 0.0 collective-permute-done.6
  566.6 0.1 pad_maximum_fusion.25
  566.7 0.2 collective-permute-done.3
  566.9 5.5 collective-permute-done.1
  572.4 0.0 collective-permute-start.5
  572.5 0.5 collective-permute-start.7
  573.0 0.1 slice_multiply_fusion.3
  573.0 0.8 collective-permute-done.5
  573.9 2.9 collective-permute-done.7
  576.8 0.2 fusion.23
  577.0 1.9 collective-permute-start.9
  579.0 3.9 collective-permute-start.8
  582.9 0.3 collective-permute-done.9
  583.2 4.0 collective-permute-done.8
  587.3 0.0 collective-permute-start.10
  587.3 0.5 collective-permute-start.11
  587.8 0.9 collective-permute-done.10
  588.7 2.9 collective-permute-done.11
  591.6 0.9 fusion.11
  (33 shorter events, 0.3 us)
Async XLA Ops:
  6.5 116.4 %copy-start = (bf16[2048,384]{1,0:T(8,128)(2,1)S(1)}, bf16[2048,384]{1,0:T(8,128)(2,1)}, u32[]{:S(2)}) copy-start(bf16[2048,384]{1,0:T(8,128)(2,1)} %param.17) | copy-start | bytes 4718596
  6.5 67.7 %copy-start.1 = (bf16[411,128]{1,0:T(8,128)(2,1)S(1)}, bf16[411,128]{1,0:T(8,128)(2,1)}, u32[]{:S(2)}) copy-start(bf16[411,128]{1,0:T(8,128)(2,1)} %param.15) | copy-start | bytes 315652
  6.5 67.7 %copy-start.6 = (f32[128]{0:T(128)S(1)}, f32[128]{0:T(128)}, u32[]{:S(2)}) copy-start(f32[128]{0:T(128)} %param.16) | copy-start | bytes 1540
  6.5 69.0 %copy-start.3 = (s32[256]{0:T(256)S(1)}, s32[256]{0:T(256)}, u32[]{:S(2)}) copy-start(s32[256]{0:T(256)} %param.14) | copy-start | bytes 3076
  6.5 116.4 %copy-start.5 = (f32[384]{0:T(512)S(1)}, f32[384]{0:T(512)}, u32[]{:S(2)}) copy-start(f32[384]{0:T(512)} %param.18) | copy-start | bytes 4612
  6.5 116.4 %copy-start.4 = (bf16[256,384]{1,0:T(8,128)(2,1)S(1)}, bf16[256,384]{1,0:T(8,128)(2,1)}, u32[]{:S(2)}) copy-start(bf16[256,384]{1,0:T(8,128)(2,1)} %param.13) | copy-start | bytes 589828
  6.6 116.4 %all-gather.4.cloned.1.call-start = ((), (), s32[]{:S(2)}) async-start(), calls=%async_computation.2 | async-start | bytes 1114112 | tf_op jit(solution)/shard_map/all_gather | solution.py:84
  75.1 117.4 %all-gather.6.cloned.1.call-start = ((), (), s32[]{:S(2)}) async-start(), calls=%async_computation.3 | async-start | bytes 3342336 | tf_op jit(solution)/shard_map/all_gather | solution.py:92
  125.6 142.8 %all-gather.8.cloned.1.call-start = ((), (), s32[]{:S(2)}) async-start(), calls=%async_computation.4 | async-start | bytes 4866048 | tf_op jit(solution)/shard_map/all_gather | solution.py:96
  126.3 268.1 %all-reduce.3.cloned.1.call-start = ((), (), s32[]{:S(2)}) async-start(), calls=%async_computation.5 | async-start | bytes 4194304 | tf_op jit(solution)/shard_map/psum | solution.py:101
  275.5 250.5 %copy-start.2 = (f32[4,32]{1,0:T(4,128)S(1)}, f32[4,32]{1,0:T(4,128)}, u32[]{:S(2)}) copy-start(f32[4,32]{1,0:T(4,128)} %param.11) | copy-start | bytes 1540
  275.5 237.9 %all-reduce.5.cloned.1.call-start = ((), (), s32[]{:S(2)}) async-start(), calls=%async_computation.6 | async-start | bytes 1048576 | tf_op jit(solution)/shard_map/psum | solution.py:113
  513.4 46.6 %all-to-all-start.1 = ((f32[32,8,411]{2,1,0:T(8,128)}), f32[32,8,411]{2,1,0:T(8,128)S(1)}, u32[]{:S(2)}, u32[]{:S(2)}) async-start(f32[32,8,411]{2,1,0:T(8,128)} %all-reduce.5.cloned.1.call-done), calls=%async_computation.1 | async-start | bytes 1048576 | tf_op jit(solution)/shard_map/all_to_all | solution.py:114
  526.1 6.1 %collective-permute-start.2 = (f32[1,32]{1,0:T(1,128)S(1)}, f32[1,32]{1,0:T(1,128)S(1)}, u32[]{:S(2)}, u32[]{:S(2)}) collective-permute-start(f32[1,32]{1,0:T(1,128)S(1)} %get-tuple-element.23), channel_id=1, source_target_pairs={{0,1},{1,2},{2,3},{3,4},{4,5},{5,6},{6,7},{7,8},{8,9},{9,10},{10,1... | collective-permute-start | bytes 392 | tf_op jit(solution)/shard_map/ppermute | solution.py:14
  529.4 7.6 %collective-permute-start = (f32[1,32]{1,0:T(1,128)S(1)}, f32[1,32]{1,0:T(1,128)S(1)}, u32[]{:S(2)}, u32[]{:S(2)}) collective-permute-start(f32[1,32]{1,0:T(1,128)S(1)} %get-tuple-element.24), channel_id=1, source_target_pairs={{1,0},{2,1},{3,2},{4,3},{5,4},{6,5},{7,6},{8,7},{9,8},{10,9},{11,1... | collective-permute-start | bytes 392 | tf_op jit(solution)/shard_map/ppermute | solution.py:15
  537.1 29.5 %collective-permute-start.4 = (f32[6,1]{1,0:T(8,128)S(1)}, f32[6,1]{1,0:T(8,128)S(1)}, u32[]{:S(2)}, u32[]{:S(2)}) collective-permute-start(f32[6,1]{1,0:T(8,128)S(1)} %get-tuple-element.13), channel_id=1, source_target_pairs={{16,0},{32,16},{48,32},{64,48},{80,64},{96,80},{112,96},{128,112},... | collective-permute-start | bytes 80 | tf_op jit(solution)/shard_map/ppermute | solution.py:15
  538.8 27.8 %collective-permute-start.6 = (f32[6,1]{1,0:T(8,128)S(1)}, f32[6,1]{1,0:T(8,128)S(1)}, u32[]{:S(2)}, u32[]{:S(2)}) collective-permute-start(f32[6,1]{1,0:T(8,128)S(1)} %get-tuple-element.14), channel_id=1, source_target_pairs={{0,16},{16,32},{32,48},{48,64},{64,80},{80,96},{96,112},{112,128},... | collective-permute-start | bytes 80 | tf_op jit(solution)/shard_map/ppermute | solution.py:14
  560.7 6.2 %collective-permute-start.3 = (f32[1,32,411]{2,1,0:T(8,128)S(1)}, f32[1,32,411]{2,1,0:T(8,128)S(1)}, u32[]{:S(2)}, u32[]{:S(2)}) collective-permute-start(f32[1,32,411]{2,1,0:T(8,128)S(1)} %mul.151), channel_id=1, source_target_pairs={{0,1},{1,2},{2,3},{3,4},{4,5},{5,6},{6,7},{7,8},{8,9},{9,10},{10,1... | collective-permute-start | bytes 157832 | tf_op jit(solution)/shard_map/ppermute | solution.py:14
  564.1 8.3 %collective-permute-start.1 = (f32[1,32,411]{2,1,0:T(8,128)S(1)}, f32[1,32,411]{2,1,0:T(8,128)S(1)}, u32[]{:S(2)}, u32[]{:S(2)}) collective-permute-start(f32[1,32,411]{2,1,0:T(8,128)S(1)} %mul.151), channel_id=1, source_target_pairs={{1,0},{2,1},{3,2},{4,3},{5,4},{6,5},{7,6},{8,7},{9,8},{10,9},{11,1... | collective-permute-start | bytes 157832 | tf_op jit(solution)/shard_map/ppermute | solution.py:15
  572.4 1.4 collective-permute-start.5
  572.5 4.3 collective-permute-start.7
  577.0 6.2 %collective-permute-start.9 = (f32[1,32,411]{2,1,0:T(8,128)S(1)}, f32[1,32,411]{2,1,0:T(8,128)S(1)}, u32[]{:S(2)}, u32[]{:S(2)}) collective-permute-start(f32[1,32,411]{2,1,0:T(8,128)S(1)} %get-tuple-element.11), channel_id=1, source_target_pairs={{0,1},{1,2},{2,3},{3,4},{4,5},{5,6},{6,7},{7,8},{8,9},{9,10},{10,1... | collective-permute-start | bytes 157832 | tf_op jit(solution)/shard_map/ppermute | solution.py:14
  579.0 8.3 %collective-permute-start.8 = (f32[1,32,411]{2,1,0:T(8,128)S(1)}, f32[1,32,411]{2,1,0:T(8,128)S(1)}, u32[]{:S(2)}, u32[]{:S(2)}) collective-permute-start(f32[1,32,411]{2,1,0:T(8,128)S(1)} %get-tuple-element.12), channel_id=1, source_target_pairs={{1,0},{2,1},{3,2},{4,3},{5,4},{6,5},{7,6},{8,7},{9,8},{10,9},{11,1... | collective-permute-start | bytes 157832 | tf_op jit(solution)/shard_map/ppermute | solution.py:15
  587.3 1.4 collective-permute-start.10
  587.3 4.3 collective-permute-start.11
Sparse Core Ops, SparseCore 0:
  75.2 47.6 all-gather.3
  125.9 66.5 all-gather.5
  194.7 73.6 all-gather.7
  275.7 118.6 all-reduce.2
  397.4 115.9 all-reduce.4
where the time goes:
time: 600 us; the launch traced here: 599 us
  waiting for transfers between devices  470 us (78%)
  blocking collectives  61.6 us (10%)
  starting transfers between devices  33 us (6%)
  between operations  13.5 us (2%)
  matrix products  12.8 us (2%)
    psum x1, waiting for transfers between devices, body(): lax.psum(lax.dot_general(weights, cotangent, (((1,), (1,)), ((), ())), pr...  119 us
    psum x1, waiting for transfers between devices, body(): summed_grad = lax.psum(part_grad, 'chan')  117 us
    all_gather x1, waiting for transfers between devices, body(): lax.all_gather(inv_cov, 'tile', axis=0, tiled=True)  75.9 us
    all_gather x1, waiting for transfers between devices, body(): all_depart = lax.all_gather(departure, 'chan', axis=1, tiled=True)  66.2 us
    all_gather x1, waiting for transfers between devices, body(): lax.all_gather(active, 'chan', axis=0, tiled=True)  47.4 us
    all_to_all x1, blocking collectives, body(): lax.all_to_all(outgoing.astype(jnp.bfloat16), 'tile', split_axis=0, conca...  35.1 us
    all_gather x1, blocking collectives, body(): lax.all_gather(columns, 'chan', axis=0, tiled=True)  26.5 us
    all_to_all x1, waiting for transfers between devices, body(): lax.all_to_all(summed_grad, 'tile', split_axis=0, concat_axis=0, tiled=True)  21.3 us
  transfers between devices with their start and end apart: 18, of which 15 were waited for; matrix products, arithmetic and copies ran while one was open for 0% of the time, Pallas kernels for 0%

commit v1 on v0

--- a/solution.py
+++ b/solution.py
@@ -2,6 +2,13 @@
 import jax.numpy as jnp
 from jax import lax
 from jax.sharding import PartitionSpec as P
+
+
+def all_by_exchange(x, mesh_axis, along):
+    count = lax.axis_size(mesh_axis)
+    blocks = jnp.stack([x for _ in range(count)])
+    blocks = lax.all_to_all(blocks, mesh_axis, split_axis=0, concat_axis=0)
+    return jnp.concatenate(blocks, axis=along)
 
 
 def padded_2(value, sides, width, wrap):
@@ -81,7 +88,7 @@
     active = (preact * squash).astype(jnp.bfloat16)
     weights = w_radiance
     radiance = lax.dot_general(
-        lax.all_gather(active, "chan", axis=0, tiled=True),
+        all_by_exchange(active, "chan", 0),
         weights,
         (((0,), (0,)), ((), ())),
         preferred_element_type=jnp.float32,

time: 600 us -> 563 us (0.938)
  waiting for transfers between devices: 470 us -> 428 us
    all_gather x1 -> x0, waiting for transfers between devices: 47.4 us -> none  [body(): lax.all_gather(active, 'chan', axis=0, tiled=True)]
    all_to_all x0 -> x1, waiting for transfers between devices: none -> 14.1 us  [all_by_exchange(): blocks = lax.all_to_all(blocks, mesh_axis, split_axis=0, concat_axis=0)]
    all_gather x1, waiting for transfers between devices: 66.2 us -> 57.9 us  [body(): all_depart = lax.all_gather(departure, 'chan', axis=1, tiled=True)]
where the time goes in v1:
time: 563 us
  waiting for transfers between devices  428 us (76%)
  blocking collectives  61.6 us (11%)
  starting transfers between devices  38.7 us (7%)
  between operations  13.5 us (2%)
  matrix products  11 us (2%)
  other arithmetic  5.88 us (1%)
    psum x1, waiting for transfers between devices, body(): lax.psum(lax.dot_general(weights, cotangent, (((1,), (1,)), ((), ())), pr...  119 us
    psum x1, waiting for transfers between devices, body(): summed_grad = lax.psum(part_grad, 'chan')  117 us
    all_gather x1, waiting for transfers between devices, body(): lax.all_gather(inv_cov, 'tile', axis=0, tiled=True)  75.9 us
    all_gather x1, waiting for transfers between devices, body(): all_depart = lax.all_gather(departure, 'chan', axis=1, tiled=True)  57.9 us
    all_to_all x1, blocking collectives, body(): lax.all_to_all(outgoing.astype(jnp.bfloat16), 'tile', split_axis=0, conca...  35.1 us
    all_gather x1, blocking collectives, body(): lax.all_gather(columns, 'chan', axis=0, tiled=True)  26.5 us
    all_to_all x1, waiting for transfers between devices, body(): lax.all_to_all(summed_grad, 'tile', split_axis=0, concat_axis=0, tiled=True)  21.3 us
    ppermute x6, waiting for transfers between devices, padded_2(): after = lax.ppermute(first, axis, down)  16.1 us
  transfers between devices with their start and end apart: 18, of which 15 were waited for; matrix products, arithmetic and copies ran while one was open for 0% of the time, Pallas kernels for 0%

profile of v1, /device:TPU:6, one launch (start us, length us, event | category | flops | bytes accessed | tf_op | source)
XLA Modules:
  0.0 562.6 jit_solution(10974468841178897335)
XLA Ops:
  6.5 0.9 copy.31
  7.5 1.0 reduce_sum.35
  8.6 3.3 convert_reduce_fusion
  11.9 26.5 %all_gather.9 = bf16[128,411]{1,0:T(8,128)(2,1)S(1)} all-gather(bf16[8,411]{1,0:T(8,128)(2,1)S(1)} %multiply_convert_fusion.3), channel_id=1, replica_groups=mesh['tile'=32,'chan'=16] {'chan'}, dimensions={0}, use_global_device_ids=true | all-gather | bytes 111792 | tf_op jit(solution)/shard_map/all_gather | solution.py:77
  38.4 0.2 dynamic-slice_reduce_fusion
  38.6 0.3 convolution_convert_fusion
  38.9 0.1 copy.34
  39.0 35.1 %all_to_all.29 = bf16[32,8,411]{2,1,0:T(8,128)(2,1)S(1)} all-to-all(bf16[32,8,411]{2,1,0:T(8,128)(2,1)S(1)} %bitcast.28), channel_id=1, replica_groups=mesh['tile'=32,'chan'=16] {'tile'}, dimensions={0} | all-to-all | bytes 420864 | tf_op jit(solution)/shard_map/all_to_all | solution.py:80
  74.2 0.0 copy-start.3
  74.2 0.2 multiply_convert_fusion.1
  74.4 0.1 copy.35
  74.5 1.1 stack.2
  75.6 5.7 %all-to-all-start.1 = ((bf16[16,128,256]{2,1,0:T(8,128)(2,1)}), bf16[16,128,256]{2,1,0:T(8,128)(2,1)S(1)}, u32[]{:S(2)}, u32[]{:S(2)}) async-start(bf16[16,128,256]{2,1,0:T(8,128)(2,1)} %stack.2), calls=%async_computation.1 | async-start | bytes 2097152 | tf_op jit(solution)/shard_map/all_to_all | solution.py:10
  81.3 0.0 all-gather.3.cloned.1.call-start
  81.3 0.2 dynamic-slice_reduce_fusion.1
  81.5 0.1 iota_compare_fusion.4
  81.6 0.1 lt.53
  81.7 14.1 %all-to-all-done.1 = bf16[16,128,256]{2,1,0:T(8,128)(2,1)S(1)} async-done(((bf16[16,128,256]{2,1,0:T(8,128)(2,1)}), bf16[16,128,256]{2,1,0:T(8,128)(2,1)S(1)}, u32[]{:S(2)}, u32[]{:S(2)}) %all-to-all-start.1) | async-done | bytes 1048608 | tf_op jit(solution)/shard_map/all_to_all | solution.py:10
  95.8 1.4 fusion.6
  97.3 0.0 all-gather.3.cloned.1.call-update
  97.3 0.0 all-gather.5.cloned.1.call-start
  97.3 0.7 all-gather.5.cloned.1.call-update
  98.1 0.0 all-reduce.3.cloned.1.call-start
  98.1 57.9 %all-gather.3.cloned.1.call-done = bf16[256,6144]{1,0:T(8,128)(2,1)} async-done(((bf16[256,384]{1,0:T(8,128)(2,1)}), bf16[256,6144]{1,0:T(8,128)(2,1)}) %all-gather.3.cloned.1.call-update) | async-done | bytes 3145744 | tf_op jit(solution)/shard_map/all_gather | solution.py:99
  156.0 75.9 %all-gather.5.cloned.1.call-done = bf16[6144,384]{1,0:T(8,128)(2,1)} async-done(((bf16[192,384]{1,0:T(8,128)(2,1)}), bf16[6144,384]{1,0:T(8,128)(2,1)}) %all-gather.5.cloned.1.call-update) | async-done | bytes 4718608 | tf_op jit(solution)/shard_map/all_gather | solution.py:103
  231.9 7.1 %convolution_bitcast_fusion = f32[2048,256]{0,1:T(8,128)} fusion(bf16[2048,384]{1,0:T(8,128)(2,1)S(1)} %copy-done, bf16[256,6144]{1,0:T(8,128)(2,1)} %all-gather.3.cloned.1.call-done, bf16[6144,384]{1,0:T(8,128)(2,1)} %all-gather.5.cloned.1.call-done), kind=kOutput, calls=%fused_computation.5 | convolution fusion | flops 1610711040 | bytes 11534336 | tf_op jit(solution)/shard_map/dot_general | solution.py:109
  239.0 0.0 all-reduce.3.cloned.1.call-update
  239.0 0.0 all-reduce.5.cloned.1.call-start
  239.1 118.8 %all-reduce.3.cloned.1.call-done = f32[2048,256]{0,1:T(8,128)} async-done(((f32[2048,256]{0,1:T(8,128)}), f32[2048,256]{0,1:T(8,128)}) %all-reduce.3.cloned.1.call-update) | async-done | bytes 2097168 | tf_op jit(solution)/shard_map/psum | solution.py:108
  357.8 1.9 convolution_bitcast_fusion.1
  359.8 0.0 all-reduce.5.cloned.1.call-update
  359.8 117.1 %all-reduce.5.cloned.1.call-done = f32[32,8,411]{2,1,0:T(8,128)} async-done(((f32[32,8,411]{2,1,0:T(8,128)}), f32[32,8,411]{2,1,0:T(8,128)}) %all-reduce.5.cloned.1.call-update) | async-done | bytes 420880 | tf_op jit(solution)/shard_map/psum | solution.py:120
  476.9 12.6 %all-to-all-start.2 = ((f32[32,8,411]{2,1,0:T(8,128)}), f32[32,8,411]{2,1,0:T(8,128)S(1)}, u32[]{:S(2)}, u32[]{:S(2)}) async-start(f32[32,8,411]{2,1,0:T(8,128)} %all-reduce.5.cloned.1.call-done), calls=%async_computation.2 | async-start | bytes 1048576 | tf_op jit(solution)/shard_map/all_to_all | solution.py:121
  489.5 3.4 collective-permute-start.2
  492.9 2.5 collective-permute-start
  495.4 0.2 dynamic-slice_reduce_fusion.2
  495.6 0.0 collective-permute-done.2
  495.6 4.8 collective-permute-done
  500.5 0.1 fusion.40
  500.6 1.7 collective-permute-start.4
  502.2 0.0 collective-permute-start.6
  502.3 21.3 %all-to-all-done.2 = f32[32,8,411]{2,1,0:T(8,128)S(1)} async-done(((f32[32,8,411]{2,1,0:T(8,128)}), f32[32,8,411]{2,1,0:T(8,128)S(1)}, u32[]{:S(2)}, u32[]{:S(2)}) %all-to-all-start.2) | async-done | bytes 420896 | tf_op jit(solution)/shard_map/all_to_all | solution.py:121
  523.5 0.6 gather_fusion
  524.1 0.1 select_multiply_fusion
  524.2 3.4 collective-permute-start.3
  527.6 2.5 collective-permute-start.1
  530.1 0.1 pad_maximum_fusion.25
  530.2 0.2 collective-permute-done.3
  530.4 5.5 collective-permute-done.1
  535.9 0.0 collective-permute-start.5
  535.9 0.5 collective-permute-start.7
  536.4 0.1 slice_multiply_fusion.3
  536.5 0.8 collective-permute-done.5
  537.3 2.9 collective-permute-done.7
  540.3 0.2 fusion.23
  540.5 1.9 collective-permute-start.9
  542.4 3.9 collective-permute-start.8
  546.4 0.3 collective-permute-done.9
  546.7 4.0 collective-permute-done.8
  550.7 0.0 collective-permute-start.10
  550.8 0.5 collective-permute-start.11
  551.3 0.9 collective-permute-done.10
  552.2 2.9 collective-permute-done.11
  555.1 0.9 fusion.11
  (34 shorter events, 0.3 us)
Async XLA Ops:
  6.5 89.3 %copy-start = (bf16[2048,384]{1,0:T(8,128)(2,1)S(1)}, bf16[2048,384]{1,0:T(8,128)(2,1)}, u32[]{:S(2)}) copy-start(bf16[2048,384]{1,0:T(8,128)(2,1)} %param.17) | copy-start | bytes 4718596
  6.5 67.6 %copy-start.2 = (bf16[411,128]{1,0:T(8,128)(2,1)S(1)}, bf16[411,128]{1,0:T(8,128)(2,1)}, u32[]{:S(2)}) copy-start(bf16[411,128]{1,0:T(8,128)(2,1)} %param.15) | copy-start | bytes 315652
  6.5 67.6 %copy-start.6 = (f32[128]{0:T(128)S(1)}, f32[128]{0:T(128)}, u32[]{:S(2)}) copy-start(f32[128]{0:T(128)} %param.16) | copy-start | bytes 1540
  74.1 7.6 %copy-start.5 = (s32[256]{0:T(256)S(1)}, s32[256]{0:T(256)}, u32[]{:S(2)}) copy-start(s32[256]{0:T(256)} %param.14) | copy-start | bytes 3076
  74.1 21.7 %copy-start.1 = (bf16[256,384]{1,0:T(8,128)(2,1)S(1)}, bf16[256,384]{1,0:T(8,128)(2,1)}, u32[]{:S(2)}) copy-start(bf16[256,384]{1,0:T(8,128)(2,1)} %param.13) | copy-start | bytes 589828
  74.2 21.7 %copy-start.3 = (f32[384]{0:T(512)S(1)}, f32[384]{0:T(512)}, u32[]{:S(2)}) copy-start(f32[384]{0:T(512)} %param.18) | copy-start | bytes 4612
  75.6 20.2 %all-to-all-start.1 = ((bf16[16,128,256]{2,1,0:T(8,128)(2,1)}), bf16[16,128,256]{2,1,0:T(8,128)(2,1)S(1)}, u32[]{:S(2)}, u32[]{:S(2)}) async-start(bf16[16,128,256]{2,1,0:T(8,128)(2,1)} %stack.2), calls=%async_computation.1 | async-start | bytes 2097152 | tf_op jit(solution)/shard_map/all_to_all | solution.py:10
  81.3 74.7 %all-gather.3.cloned.1.call-start = ((), (), s32[]{:S(2)}) async-start(), calls=%async_computation.3 | async-start | bytes 3342336 | tf_op jit(solution)/shard_map/all_gather | solution.py:99
  97.3 134.6 %all-gather.5.cloned.1.call-start = ((), (), s32[]{:S(2)}) async-start(), calls=%async_computation.4 | async-start | bytes 4866048 | tf_op jit(solution)/shard_map/all_gather | solution.py:103
  98.1 259.8 %all-reduce.3.cloned.1.call-start = ((), (), s32[]{:S(2)}) async-start(), calls=%async_computation.5 | async-start | bytes 4194304 | tf_op jit(solution)/shard_map/psum | solution.py:108
  239.0 250.5 %copy-start.4 = (f32[4,32]{1,0:T(4,128)S(1)}, f32[4,32]{1,0:T(4,128)}, u32[]{:S(2)}) copy-start(f32[4,32]{1,0:T(4,128)} %param.11) | copy-start | bytes 1540
  239.0 237.9 %all-reduce.5.cloned.1.call-start = ((), (), s32[]{:S(2)}) async-start(), calls=%async_computation.6 | async-start | bytes 1048576 | tf_op jit(solution)/shard_map/psum | solution.py:120
  476.9 46.6 %all-to-all-start.2 = ((f32[32,8,411]{2,1,0:T(8,128)}), f32[32,8,411]{2,1,0:T(8,128)S(1)}, u32[]{:S(2)}, u32[]{:S(2)}) async-start(f32[32,8,411]{2,1,0:T(8,128)} %all-reduce.5.cloned.1.call-done), calls=%async_computation.2 | async-start | bytes 1048576 | tf_op jit(solution)/shard_map/all_to_all | solution.py:121
  489.5 6.1 %collective-permute-start.2 = (f32[1,32]{1,0:T(1,128)S(1)}, f32[1,32]{1,0:T(1,128)S(1)}, u32[]{:S(2)}, u32[]{:S(2)}) collective-permute-start(f32[1,32]{1,0:T(1,128)S(1)} %get-tuple-element.23), channel_id=1, source_target_pairs={{0,1},{1,2},{2,3},{3,4},{4,5},{5,6},{6,7},{7,8},{8,9},{9,10},{10,1... | collective-permute-start | bytes 392 | tf_op jit(solution)/shard_map/ppermute | solution.py:21
  492.9 7.6 %collective-permute-start = (f32[1,32]{1,0:T(1,128)S(1)}, f32[1,32]{1,0:T(1,128)S(1)}, u32[]{:S(2)}, u32[]{:S(2)}) collective-permute-start(f32[1,32]{1,0:T(1,128)S(1)} %get-tuple-element.24), channel_id=1, source_target_pairs={{1,0},{2,1},{3,2},{4,3},{5,4},{6,5},{7,6},{8,7},{9,8},{10,9},{11,1... | collective-permute-start | bytes 392 | tf_op jit(solution)/shard_map/ppermute | solution.py:22
  500.6 29.5 %collective-permute-start.4 = (f32[6,1]{1,0:T(8,128)S(1)}, f32[6,1]{1,0:T(8,128)S(1)}, u32[]{:S(2)}, u32[]{:S(2)}) collective-permute-start(f32[6,1]{1,0:T(8,128)S(1)} %get-tuple-element.13), channel_id=1, source_target_pairs={{16,0},{32,16},{48,32},{64,48},{80,64},{96,80},{112,96},{128,112},... | collective-permute-start | bytes 80 | tf_op jit(solution)/shard_map/ppermute | solution.py:22
  502.2 27.8 %collective-permute-start.6 = (f32[6,1]{1,0:T(8,128)S(1)}, f32[6,1]{1,0:T(8,128)S(1)}, u32[]{:S(2)}, u32[]{:S(2)}) collective-permute-start(f32[6,1]{1,0:T(8,128)S(1)} %get-tuple-element.14), channel_id=1, source_target_pairs={{0,16},{16,32},{32,48},{48,64},{64,80},{80,96},{96,112},{112,128},... | collective-permute-start | bytes 80 | tf_op jit(solution)/shard_map/ppermute | solution.py:21
  524.2 6.2 %collective-permute-start.3 = (f32[1,32,411]{2,1,0:T(8,128)S(1)}, f32[1,32,411]{2,1,0:T(8,128)S(1)}, u32[]{:S(2)}, u32[]{:S(2)}) collective-permute-start(f32[1,32,411]{2,1,0:T(8,128)S(1)} %mul.151), channel_id=1, source_target_pairs={{0,1},{1,2},{2,3},{3,4},{4,5},{5,6},{6,7},{7,8},{8,9},{9,10},{10,1... | collective-permute-start | bytes 157832 | tf_op jit(solution)/shard_map/ppermute | solution.py:21
  527.6 8.3 %collective-permute-start.1 = (f32[1,32,411]{2,1,0:T(8,128)S(1)}, f32[1,32,411]{2,1,0:T(8,128)S(1)}, u32[]{:S(2)}, u32[]{:S(2)}) collective-permute-start(f32[1,32,411]{2,1,0:T(8,128)S(1)} %mul.151), channel_id=1, source_target_pairs={{1,0},{2,1},{3,2},{4,3},{5,4},{6,5},{7,6},{8,7},{9,8},{10,9},{11,1... | collective-permute-start | bytes 157832 | tf_op jit(solution)/shard_map/ppermute | solution.py:22
  535.9 1.4 collective-permute-start.5
  535.9 4.3 collective-permute-start.7
  540.5 6.2 %collective-permute-start.9 = (f32[1,32,411]{2,1,0:T(8,128)S(1)}, f32[1,32,411]{2,1,0:T(8,128)S(1)}, u32[]{:S(2)}, u32[]{:S(2)}) collective-permute-start(f32[1,32,411]{2,1,0:T(8,128)S(1)} %get-tuple-element.11), channel_id=1, source_target_pairs={{0,1},{1,2},{2,3},{3,4},{4,5},{5,6},{6,7},{7,8},{8,9},{9,10},{10,1... | collective-permute-start | bytes 157832 | tf_op jit(solution)/shard_map/ppermute | solution.py:21
  542.4 8.3 %collective-permute-start.8 = (f32[1,32,411]{2,1,0:T(8,128)S(1)}, f32[1,32,411]{2,1,0:T(8,128)S(1)}, u32[]{:S(2)}, u32[]{:S(2)}) collective-permute-start(f32[1,32,411]{2,1,0:T(8,128)S(1)} %get-tuple-element.12), channel_id=1, source_target_pairs={{1,0},{2,1},{3,2},{4,3},{5,4},{6,5},{7,6},{8,7},{9,8},{10,9},{11,1... | collective-permute-start | bytes 157832 | tf_op jit(solution)/shard_map/ppermute | solution.py:22
  550.7 1.4 collective-permute-start.10
  550.8 4.3 collective-permute-start.11
Sparse Core Ops, SparseCore 0:
  97.4 58.5 all-gather.2
  158.1 73.6 all-gather.4
  239.1 118.6 all-reduce.2
  360.9 115.9 all-reduce.4
